TPU v7x, 32 devices: a whole 2x2x4 slice. The times are simulated.
32 devices in a mesh: grp: 8 (over y, x, core), blk: 4 (over z).
Axes of the slice: x: 2, y: 2, z: 4, core: 2. Of those that a mesh axis runs over, the one named last changes fastest.
Arguments:
- a_blocks: bfloat16 [1024, 24, 4096], P(('grp', 'blk')), may hold values from -0.25 to 0.25
- a_cols: int32 [1024, 24], P(('grp', 'blk')), may hold values from 0 to 127, as said below
- p_blocks: bfloat16 [1024, 3, 4096], P(('grp', 'blk')), may hold values from -1 to 1
- p_cols: int32 [1024, 3], P('grp'), may hold values from 0 to 31, as said below
- owner: int32 [4, 8, 8], P('blk'), may hold values from 0 to 7, as said below
Outputs:
- coarse_out: bfloat16 [256, 11, 4096], P(('grp', 'blk'))
Inputs may be any that keep to these rules, and one draw needn't show every extreme that they name: `a_cols`: the first block of each fine row is its diagonal block; every other block's row has an aggregate at cyclic distance at most 1 from the row's aggregate over the group's 32 aggregates; a column may repeat, and repeated blocks add. `p_cols`: the first block of each fine row is its aggregate; the group's fine rows b * 32 to (b + 1) * 32 - 1 hold exactly the aggregates b * 8 to (b + 1) * 8 - 1, 4 rows each; the other two are distinct aggregates at cyclic distance 1 or 2 from it. `owner`: for each blk index and group, the 8 coarse rows go to distinct grp indices.
All inputs are finite; a program needn't handle non-finite values.
Results may differ from a plain program's by a relative error of at most 0.0053.
Values may be sent and summed in bfloat16 or wider, within the bound.
No kernel may reach another device: no remote copies, remote signals or barrier semaphores. Data moves between devices by JAX's collectives and lax.ppermute only.
A program may use at most 128 MiB of HBM per device.

v0:
```python
import jax
import jax.numpy as jnp
from jax import lax
from jax.sharding import PartitionSpec as P

B = 64
BC = 64
RATIO = 4
SPREAD = 7
BAND = 11


def padded_2(cells, sides, width):
    for axis, dim in sides:
        count = lax.axis_size(axis)
        head = lax.slice_in_dim(cells, 0, width, axis=dim)
        tail = lax.slice_in_dim(cells, cells.shape[dim] - width, cells.shape[dim], axis=dim)
        cells = jnp.concatenate(
            [
                lax.ppermute(tail, axis, [(i, (i + 1) % count) for i in range(count)]),
                cells,
                lax.ppermute(head, axis, [((i + 1) % count, i) for i in range(count)]),
            ],
            axis=dim,
        )
    return cells


def from_behind(block, axis, distance):
    devices = range(lax.axis_size(axis))
    route = [((i - distance) % len(devices), i) for i in devices]
    return lax.ppermute(block, axis, route)


def cyclic(value, modulus):
    return (value + modulus // 2) % modulus - modulus // 2


def body(a_blocks, a_cols, p_blocks, p_cols, owner):
    row_count = a_blocks.shape[0]
    loop_size = lax.axis_size("blk")
    my_place = lax.axis_index("blk")
    coarse_dev = row_count // RATIO
    coarse_all = coarse_dev * loop_size
    fine_all = row_count * loop_size
    window_rows = 3 * row_count
    padded = padded_2(p_blocks, (("blk", 0),), row_count)
    first_row = (my_place - 1) * row_count % fine_all
    doubled = jnp.concatenate([p_cols, p_cols], axis=0)
    window_cols = lax.dynamic_slice_in_dim(doubled, first_row, window_rows, 0)
    base_aggregate = (my_place - 1) * coarse_dev % coarse_all
    window_agg = (window_cols[:, 0] - base_aggregate) % coarse_all
    positions = jnp.arange(window_rows, dtype=jnp.int32)
    earlier = (window_agg[:, None] == window_agg[None, :]) & (
        positions[None, :] < positions[:, None]
    )
    member = jnp.sum(earlier.astype(jnp.int32), axis=1)
    destination = window_agg * RATIO + member
    slot_five = cyclic(window_cols - window_cols[:, :1], coarse_all) + 2
    five_hot = (slot_five[..., None] == jnp.arange(5, dtype=jnp.int32)).astype(jnp.bfloat16)
    selected = jnp.einsum(
        "jms,jmx->jsx", five_hot, padded, preferred_element_type=jnp.float32
    ).astype(jnp.bfloat16)
    row_order = (destination[:, None] == positions[None, :]).astype(jnp.bfloat16)
    ordered = jnp.einsum(
        "jd,jsx->dsx", row_order, selected, preferred_element_type=jnp.float32
    ).astype(jnp.bfloat16)
    ordered = ordered.reshape(3 * coarse_dev, RATIO, 5, B, BC)
    local_agg = window_agg[row_count : 2 * row_count]
    local_dest = destination[row_count : 2 * row_count] - row_count
    far_rows = (a_cols - first_row) % fine_all
    far_agg = window_agg[far_rows]
    far_member = member[far_rows]
    twelve = (far_agg - local_agg[:, None] + 1) * RATIO + far_member
    twelve_hot = (twelve[..., None] == jnp.arange(3 * RATIO, dtype=jnp.int32)).astype(jnp.bfloat16)
    merged = jnp.einsum("fks,fkx->fsx", twelve_hot, a_blocks, preferred_element_type=jnp.float32)
    local_order = (local_dest[:, None] == jnp.arange(row_count, dtype=jnp.int32)[None, :]).astype(
        jnp.float32
    )
    a_ordered = jnp.einsum("fd,fsx->dsx", local_order, merged, precision=lax.Precision.HIGHEST)
    a_ordered = a_ordered.reshape(coarse_dev, RATIO, 3, RATIO, B, B)
    p_window = jnp.stack(
        [ordered[coarse_dev - 1 + near : 2 * coarse_dev - 1 + near] for near in range(3)], axis=1
    )
    products = jnp.einsum(
        "cidtab,cdtsbx->cidsax",
        a_ordered,
        p_window.astype(jnp.float32),
        precision=lax.Precision.HIGHEST,
    )
    ap_sum = jnp.pad(products[:, :, 0], ((0, 0), (0, 0), (0, 2), (0, 0), (0, 0)))
    ap_sum = ap_sum + jnp.pad(products[:, :, 1], ((0, 0), (0, 0), (1, 1), (0, 0), (0, 0)))
    ap_sum = ap_sum + jnp.pad(products[:, :, 2], ((0, 0), (0, 0), (2, 0), (0, 0), (0, 0)))
    ap_rows = ap_sum.astype(jnp.bfloat16)
    own_p = ordered[coarse_dev : 2 * coarse_dev]
    blocks_out = jnp.einsum(
        "cisbu,ciebv->cseuv", own_p, ap_rows, preferred_element_type=jnp.float32
    )
    blocks_out = blocks_out.reshape(coarse_dev, 5, SPREAD, BC * BC)
    partial_value = jnp.pad(blocks_out[:, 0], ((coarse_dev - 2, coarse_dev + 2), (4, 0), (0, 0)))
    for upper in range(1, 5):
        partial_value = partial_value + jnp.pad(
            blocks_out[:, upper],
            ((coarse_dev + upper - 2, coarse_dev - upper + 2), (4 - upper, upper), (0, 0)),
        )
    rounded = partial_value.astype(jnp.bfloat16).reshape(3, coarse_dev, BAND, BC * BC)
    from_before = from_behind(rounded[2], "blk", 1)
    from_after = from_behind(rounded[0], "blk", -1)
    reduced = (
        rounded[1].astype(jnp.float32)
        + from_before.astype(jnp.float32)
        + from_after.astype(jnp.float32)
    ).astype(jnp.bfloat16)
    owner_here = owner[0]
    group_count = lax.axis_size("grp")
    my_group = lax.axis_index("grp")
    targets_here = owner_here[my_group]
    chosen_mask = targets_here[None, :] == jnp.arange(group_count, dtype=jnp.int32)[:, None]
    outgoing = jnp.where(chosen_mask[:, :, None, None], reduced[None], jnp.zeros((), jnp.bfloat16))
    outgoing = jnp.sum(outgoing, axis=1, dtype=jnp.float32).astype(jnp.bfloat16)
    result = lax.all_to_all(outgoing, "grp", split_axis=0, concat_axis=0, tiled=True)
    return result


def solution(mesh):
    return jax.shard_map(
        body,
        mesh=mesh,
        in_specs=(
            P(("grp", "blk"), None, None),
            P(("grp", "blk"), None),
            P(("grp", "blk"), None, None),
            P("grp", None),
            P("blk", None, None),
        ),
        out_specs=P(("grp", "blk"), None, None),
        check_vma=False,
    )
```

profile of v0, /device:TPU:0, one launch (start us, length us, event | category | flops | bytes accessed | tf_op | source)
XLA Modules:
  0.0 206.3 jit_solution(3045447607678544224)
XLA Ops:
  0.0 3.1 %collective-permute-start = (bf16[32,3,4096]{2,0,1:T(8,128)(2,1)}, bf16[32,3,4096]{2,0,1:T(8,128)(2,1)S(1)}, u32[]{:S(2)}, u32[]{:S(2)}) collective-permute-start(bf16[32,3,4096]{2,0,1:T(8,128)(2,1)} %param.7), channel_id=1, source_target_pairs={{0,1},{1,2},{2,3},{3,0},{4,5},{5,6},{6,7},{7,4},{8,9},{9,10},{10,1... | collective-permute-start | bytes 2359304 | tf_op jit(solution)/shard_map/ppermute | solution.py:20
  7.2 4.8 %gather_fusion = s32[768]{0:T(1024)S(1)} fusion(s32[96]{0:T(128)S(1)} %and_select_fusion, s32[1024]{0:T(1024)S(1)} %pad_clamp_fusion), kind=kCustom, calls=%fused_computation | custom fusion | bytes 9216 | tf_op jit(solution)/shard_map/gather | solution.py:72
  12.0 4.8 %gather_fusion.1 = s32[768]{0:T(1024)S(1)} fusion(s32[96]{0:T(128)S(1)} %convert_reduce_fusion, s32[1024]{0:T(1024)S(1)} %pad_clamp_fusion), kind=kCustom, calls=%fused_computation.1 | custom fusion | bytes 9216 | tf_op jit(solution)/shard_map/gather | solution.py:73
  17.8 4.3 %fusion.24 = f32[32,12,4096]{2,1,0:T(8,128)S(1)} fusion(bf16[32,24,4096]{2,1,0:T(8,128)(2,1)} %param.5, s32[32,24]{1,0:T(8,128)S(1)} %multiply_add_fusion), kind=kOutput, calls=%fused_computation.37 | convolution fusion | flops 75506688 | bytes 12585984 | tf_op jit(solution)/shard_map/fks,fkx->fsx/dot_general | solution.py:76
  22.1 8.0 %fusion.9 = f32[32,12,4096]{2,0,1:T(8,128)} fusion(f32[32,12,4096]{2,1,0:T(8,128)S(1)} %fusion.24, s32[32]{0:T(128)S(1)} %slice_add_fusion), kind=kOutput, calls=%fused_computation.12 | convolution fusion | flops 603980800 | bytes 12583040 | tf_op jit(solution)/shard_map/fd,fsx->dsx/dot_general | solution.py:80
  30.1 10.9 %reshape.85 = f32[8,4,3,4,64,64]{5,4,1,0,3,2:T(8,128)} reshape(f32[32,12,4096]{2,0,1:T(8,128)} %fusion.9) | data formatting | bytes 12582912 | tf_op jit(solution)/shard_map/reshape | solution.py:81
  42.6 6.4 %convolution_convert_fusion = bf16[96,5,4096]{2,1,0:T(8,128)(2,1)S(1)} fusion(bf16[32,3,4096]{2,1,0:T(4,128)(2,1)S(1)} %copy.62, bf16[32,3,4096]{2,1,0:T(4,128)(2,1)S(1)} %copy.61, bf16[32,3,4096]{2,1,0:T(4,128)(2,1)S(1)} %copy.60, s32[96,3]{1,0:T(8,128)S(1)} %copy.59), kind=kOutput, calls=%fused_computation.11 | convolution fusion | flops 20841888 | bytes 6292608 | tf_op jit(solution)/shard_map/jms,jmx->jsx/dot_general | solution.py:61
  49.0 5.0 %convolution_convert_fusion.1 = bf16[96,5,4096]{2,0,1:T(8,128)(2,1)S(1)} fusion(bf16[96,5,4096]{2,1,0:T(8,128)(2,1)S(1)} %convolution_convert_fusion, s32[96]{0:T(128)S(1)} %fusion.41), kind=kOutput, calls=%fused_computation.14 | convolution fusion | flops 379462656 | bytes 7864704 | tf_op jit(solution)/shard_map/jd,jsx->dsx/dot_general | solution.py:65
  56.1 3.9 %stack.13 = bf16[8,1,4,5,64,64]{5,4,2,0,3,1:T(8,128)(2,1)} reshape(bf16[32,5,4096]{2,0,1:T(8,128)(2,1)S(1)} %get-tuple-element.15) | data formatting | bytes 2621440 | tf_op jit(solution)/shard_map/stack | solution.py:82
  60.1 3.9 %slice.70 = bf16[8,4,5,64,64]{4,3,1,0,2:T(8,128)(2,1)} reshape(bf16[32,5,4096]{2,0,1:T(8,128)(2,1)S(1)} %get-tuple-element.15) | data formatting | bytes 2621440 | tf_op jit(solution)/shard_map/slice | solution.py:83
  63.9 5.0 %stack.12 = bf16[8,1,4,5,64,64]{5,4,2,0,3,1:T(8,128)(2,1)} reshape(bf16[32,5,4096]{2,0,1:T(8,128)(2,1)} %get-tuple-element.13) | data formatting | bytes 2621440 | tf_op jit(solution)/shard_map/stack | solution.py:82
  68.9 4.4 %copy.64 = bf16[8,1,4,5,64,64]{4,5,2,3,1,0:T(8,128)(2,1)} copy(bf16[8,1,4,5,64,64]{5,4,2,0,3,1:T(8,128)(2,1)} %stack.12) | data formatting | bytes 2621440 | tf_op jit(solution)/shard_map/stack | solution.py:82
  75.9 3.8 %stack.14 = bf16[8,1,4,5,64,64]{5,4,2,0,3,1:T(8,128)(2,1)S(1)} reshape(bf16[32,5,4096]{2,0,1:T(8,128)(2,1)} %get-tuple-element.14) | data formatting | bytes 2621440 | tf_op jit(solution)/shard_map/stack | solution.py:82
  79.8 2.6 %copy.66 = bf16[8,1,4,5,64,64]{4,5,2,3,1,0:T(8,128)(2,1)} copy(bf16[8,1,4,5,64,64]{5,4,2,0,3,1:T(8,128)(2,1)S(1)} %stack.14) | data formatting | bytes 2621440 | tf_op jit(solution)/shard_map/stack | solution.py:82
  82.4 18.5 %fusion.2 = f32[8,4,3,5,64,64]{4,5,1,3,2,0:T(8,128)} fusion(bf16[8,1,4,5,64,64]{4,5,2,3,1,0:T(8,128)(2,1)} %copy.66, bf16[8,1,4,5,64,64]{4,5,2,3,1,0:T(8,128)(2,1)} %copy.65, bf16[8,1,4,5,64,64]{4,5,2,3,1,0:T(8,128)(2,1)} %copy.64, f32[8,4,3,4,64,64]{5,4,1,0,3,2:T(8,128)} %reshape.85), kind=kOutput, calls=%fused_computation.4 | convolution fusion | flops 6051594240 | bytes 18087936 | tf_op jit(solution)/shard_map/cidtab,cdtsbx->cidsax/dot_general | solution.py:85
  100.9 12.5 %slice_bitcast_fusion.2 = (f32[8,4,5,64,64]{3,4,1,2,0:T(8,128)}, f32[8,4,5,64,64]{3,4,1,2,0:T(8,128)}, f32[8,4,5,64,64]{3,4,1,2,0:T(8,128)}) fusion(f32[8,4,3,5,64,64]{4,5,1,3,2,0:T(8,128)} %fusion.2), kind=kLoop, calls=%fused_computation.18 | loop fusion | bytes 15728640 | tf_op jit(solution)/shard_map/squeeze | solution.py:91
  113.4 10.9 %fusion.15 = f32[8,5,7,64,64]{3,4,1,2,0:T(8,128)} fusion(f32[8,4,5,64,64]{3,4,1,2,0:T(8,128)} %get-tuple-element.6, f32[8,4,5,64,64]{3,4,1,2,0:T(8,128)} %get-tuple-element.7, f32[8,4,5,64,64]{3,4,1,2,0:T(8,128)} %get-tuple-element.5, bf16[8,4,5,64,64]{4,3,1,0,2:T(8,128)(2,1)S(1)} %copy-done.2), kind=kOutput, calls=%fused_computation.23 | convolution fusion | flops 589955072 | bytes 13762560 | tf_op jit(solution)/shard_map/cisbu,ciebv->cseuv/dot_general | solution.py:96
  124.3 10.9 %copy.73 = f32[8,5,7,64,64]{4,3,0,2,1:T(8,128)} copy(f32[8,5,7,64,64]{3,4,1,2,0:T(8,128)} %fusion.15) | data formatting | bytes 9175040 | tf_op jit(solution)/shard_map/cisbu,ciebv->cseuv/transpose | solution.py:96
  135.2 8.2 %reshape.86 = f32[8,5,7,4096]{3,0,2,1:T(8,128)} reshape(f32[8,5,7,64,64]{4,3,0,2,1:T(8,128)} %copy.73) | data formatting | bytes 9175040 | tf_op jit(solution)/shard_map/reshape | solution.py:99
  147.9 3.8 %collective-permute-start.3 = (bf16[8,11,4096]{2,0,1:T(8,128)(2,1)}, bf16[8,11,4096]{2,0,1:T(8,128)(2,1)}, u32[]{:S(2)}, u32[]{:S(2)}) collective-permute-start(bf16[8,11,4096]{2,0,1:T(8,128)(2,1)} %get-tuple-element.17), channel_id=1, source_target_pairs={{1,0},{2,1},{3,2},{0,3},{5,4},{6,5},{7,6},{4,7},{9,8},{10,9},{11,1... | collective-permute-start | bytes 2162696 | tf_op jit(solution)/shard_map/ppermute | solution.py:32
  151.8 17.2 %collective-permute-done.2 = bf16[8,11,4096]{2,0,1:T(8,128)(2,1)S(1)} collective-permute-done((bf16[8,11,4096]{2,0,1:T(8,128)(2,1)}, bf16[8,11,4096]{2,0,1:T(8,128)(2,1)S(1)}, u32[]{:S(2)}, u32[]{:S(2)}) %collective-permute-start.2) | collective-permute-done | bytes 720928 | tf_op jit(solution)/shard_map/ppermute | solution.py:32
  169.0 12.3 %collective-permute-done.3 = bf16[8,11,4096]{2,0,1:T(8,128)(2,1)} collective-permute-done((bf16[8,11,4096]{2,0,1:T(8,128)(2,1)}, bf16[8,11,4096]{2,0,1:T(8,128)(2,1)}, u32[]{:S(2)}, u32[]{:S(2)}) %collective-permute-start.3) | collective-permute-done | bytes 720928 | tf_op jit(solution)/shard_map/ppermute | solution.py:32
  182.8 3.3 %select_reduce_fusion = bf16[8,11,4096]{2,1,0:T(8,128)(2,1)S(1)} fusion(pred[8,8]{1,0:T(8,128)(4,1)S(1)} %iota_compare_fusion.7, bf16[8,11,4096]{2,0,1:T(8,128)(2,1)S(1)} %add_convert_fusion.2), kind=kLoop, calls=%fused_computation.15 | loop fusion | flops 5406720 | bytes 1441856 | tf_op jit(solution)/shard_map/reduce_sum | solution.py:120
  186.1 18.8 %all_to_all.5 = bf16[8,11,4096]{2,1,0:T(8,128)(2,1)S(1)} all-to-all(bf16[8,11,4096]{2,1,0:T(8,128)(2,1)S(1)} %select_reduce_fusion), channel_id=1, replica_groups=mesh['grp'=8,'blk'=4] {'grp'}, dimensions={0} | all-to-all | bytes 1441792 | tf_op jit(solution)/shard_map/all_to_all | solution.py:121
  (43 shorter events, 18.7 us)
Async XLA Ops:
  0.0 151.8 %copy-start = (s32[1,8,8]{2,1,0:T(8,128)S(1)}, s32[1,8,8]{2,1,0:T(8,128)}, u32[]{:S(2)}) copy-start(s32[1,8,8]{2,1,0:T(8,128)} %param.9) | copy-start | bytes 772
  0.0 41.2 %collective-permute-start = (bf16[32,3,4096]{2,0,1:T(8,128)(2,1)}, bf16[32,3,4096]{2,0,1:T(8,128)(2,1)S(1)}, u32[]{:S(2)}, u32[]{:S(2)}) collective-permute-start(bf16[32,3,4096]{2,0,1:T(8,128)(2,1)} %param.7), channel_id=1, source_target_pairs={{0,1},{1,2},{2,3},{3,0},{4,5},{5,6},{6,7},{7,4},{8,9},{9,10},{10,1... | collective-permute-start | bytes 2359304 | tf_op jit(solution)/shard_map/ppermute | solution.py:20
  3.1 38.8 %collective-permute-start.1 = (bf16[32,3,4096]{2,0,1:T(8,128)(2,1)}, bf16[32,3,4096]{2,0,1:T(8,128)(2,1)S(1)}, u32[]{:S(2)}, u32[]{:S(2)}) collective-permute-start(bf16[32,3,4096]{2,0,1:T(8,128)(2,1)} %param.7), channel_id=1, source_target_pairs={{1,0},{2,1},{3,2},{0,3},{5,4},{6,5},{7,6},{4,7},{9,8},{10,9},{11,1... | collective-permute-start | bytes 2359304 | tf_op jit(solution)/shard_map/ppermute | solution.py:22
  11.9 4.8 %copy-start.3 = (bf16[32,3,4096]{2,0,1:T(8,128)(2,1)S(1)}, bf16[32,3,4096]{2,0,1:T(8,128)(2,1)}, u32[]{:S(2)}) copy-start(bf16[32,3,4096]{2,0,1:T(8,128)(2,1)} %param.7) | copy-start | bytes 2359300
  30.1 10.9 %copy-start.4 = (s32[128,3]{0,1:T(4,128)S(1)}, s32[128,3]{0,1:T(4,128)}, u32[]{:S(2)}) copy-start(s32[128,3]{0,1:T(4,128)} %param.8) | copy-start | bytes 4612
  63.9 9.4 %copy-start.1 = (bf16[8,1,4,5,64,64]{5,4,2,0,3,1:T(8,128)(2,1)S(1)}, bf16[8,1,4,5,64,64]{5,4,2,0,3,1:T(8,128)(2,1)}, u32[]{:S(2)}) copy-start(bf16[8,1,4,5,64,64]{5,4,2,0,3,1:T(8,128)(2,1)} %stack.13) | copy-start | bytes 3932164
  100.9 12.6 %copy-start.2 = (bf16[8,4,5,64,64]{4,3,1,0,2:T(8,128)(2,1)S(1)}, bf16[8,4,5,64,64]{4,3,1,0,2:T(8,128)(2,1)}, u32[]{:S(2)}) copy-start(bf16[8,4,5,64,64]{4,3,1,0,2:T(8,128)(2,1)} %slice.70) | copy-start | bytes 3932164
  147.9 21.0 %collective-permute-start.2 = (bf16[8,11,4096]{2,0,1:T(8,128)(2,1)}, bf16[8,11,4096]{2,0,1:T(8,128)(2,1)S(1)}, u32[]{:S(2)}, u32[]{:S(2)}) collective-permute-start(bf16[8,11,4096]{2,0,1:T(8,128)(2,1)} %get-tuple-element.16), channel_id=1, source_target_pairs={{3,0},{0,1},{1,2},{2,3},{7,4},{4,5},{5,6},{6,7},{11,8},{8,9},{9,10... | collective-permute-start | bytes 2162696 | tf_op jit(solution)/shard_map/ppermute | solution.py:32
  147.9 33.4 %collective-permute-start.3 = (bf16[8,11,4096]{2,0,1:T(8,128)(2,1)}, bf16[8,11,4096]{2,0,1:T(8,128)(2,1)}, u32[]{:S(2)}, u32[]{:S(2)}) collective-permute-start(bf16[8,11,4096]{2,0,1:T(8,128)(2,1)} %get-tuple-element.17), channel_id=1, source_target_pairs={{1,0},{2,1},{3,2},{0,3},{5,4},{6,5},{7,6},{4,7},{9,8},{10,9},{11,1... | collective-permute-start | bytes 2162696 | tf_op jit(solution)/shard_map/ppermute | solution.py:32
where the time goes:
time: 207 us; the launch traced here: 206 us
  local copies, waits for them, and re-layouts  88.2 us (43%)
  matrix products  53 us (26%)
  waiting for transfers between devices  29.5 us (14%)
  blocking collectives  18.8 us (9%)
  starting transfers between devices  8.96 us (4%)
  other arithmetic  7.52 us (4%)
    ppermute x2, waiting for transfers between devices, from_behind(): return lax.ppermute(block, axis, route)  29.5 us
    another operation x6, local copies, waits for them, and re-layouts, body(): jnp.stack([ordered[coarse_dev - 1 + near:2 * coarse_dev - 1 + near] for n...  22.3 us
    all_to_all x1, blocking collectives, body(): lax.all_to_all(outgoing, 'grp', split_axis=0, concat_axis=0, tiled=True)  18.8 us
    dot_general x1, matrix products, body(): jnp.einsum('cidtab,cdtsbx->cidsax', a_ordered, p_window.astype(jnp.float3...  18.5 us
    squeeze x1, local copies, waits for them, and re-layouts, body(): products[:, :, 0]  12.5 us
    transpose x1, local copies, waits for them, and re-layouts, body(): jnp.einsum('cisbu,ciebv->cseuv', own_p, ap_rows, preferred_element_type=j...  10.9 us
    reshape x1, local copies, waits for them, and re-layouts, body(): a_ordered = a_ordered.reshape(coarse_dev, RATIO, 3, RATIO, B, B)  10.9 us
    dot_general x1, matrix products, body(): jnp.einsum('cisbu,ciebv->cseuv', own_p, ap_rows, preferred_element_type=j...  10.9 us
  transfers between devices with their start and end apart: 4, of which 2 were waited for; matrix products, arithmetic and copies ran while one was open for 18% of the time, Pallas kernels for 0%

commit v1 on v0

v1 whole, which is shorter than its diff:
```python
import functools

import jax
import jax.numpy as jnp
from jax import lax
from jax.experimental import pallas as pl
from jax.experimental.pallas import tpu as pltpu
from jax.sharding import PartitionSpec as P

RATIO = 4
REACH = 2
F32 = jnp.float32
BF16 = jnp.bfloat16
LIMIT = 40 * 1024 * 1024


def iota(shape, axis):
    return lax.broadcasted_iota(jnp.int32, shape, axis)


def rows_sum(values):
    return jnp.sum(values.astype(F32), axis=0, keepdims=True)


def lanes_sum(values):
    return jnp.sum(values.astype(F32), axis=1, keepdims=True)


def wrapped(values, modulus):
    half = modulus // 2
    values = jnp.where(values >= half, values - modulus, values)
    return jnp.where(values < -half, values + modulus, values)


def places(cols_ref, mine, rows):
    group = cols_ref.shape[1]
    agg_row = cols_ref[0:1, :].astype(F32)
    sub, lane = iota((group, group), 0), iota((group, group), 1)
    agg_wide = jnp.broadcast_to(agg_row, (group, group))
    agg_col = lanes_sum(jnp.where(sub == lane, agg_wide, 0.0))
    same = agg_wide == agg_col
    member_row = rows_sum(jnp.where(same & (sub < lane), 1.0, 0.0))
    member_col = lanes_sum(jnp.where(same & (lane < sub), 1.0, 0.0))
    base = (mine * rows).astype(F32)
    place_row = wrapped(agg_row * RATIO + member_row - base, group)
    place_col = wrapped(agg_col * RATIO + member_col - base, group)
    return place_row, place_col


def column_rel(cols_ref, mine, coarse):
    total = cols_ref.shape[1] // RATIO
    cols = cols_ref[...].astype(F32)
    near = wrapped(cols - cols[0:1, :], total)
    own = wrapped(cols[0:1, :] - (mine * coarse).astype(F32), total)
    return own + near


def own_lanes(values, mine, rows):
    group = values.shape[1]
    values = jnp.broadcast_to(values, (8, group))
    return pltpu.roll(values, (group - mine * rows) % group, 1)[:, :128]


def three_wide(pieces, rows):
    lane = iota((8, 128), 1)
    out = jnp.full((8, 128), -1.0, F32)
    for m, piece in enumerate(pieces):
        moved = piece if m == 0 else pltpu.roll(piece, m * rows, 1)
        out = jnp.where((lane >= m * rows) & (lane < (m + 1) * rows), moved, out)
    return out


def onehot(code, count):
    hit = iota((count, code.shape[1]), 0).astype(F32) == code
    return jnp.where(hit, 1.0, 0.0).astype(BF16)


def dot(a, b):
    return jnp.dot(a, b, preferred_element_type=F32)


def swap_halves(first, second):
    low = iota(first.shape, 1) < 64
    even = jnp.where(low, first, pltpu.roll(second, 64, 1))
    odd = jnp.where(low, pltpu.roll(first, 64, 1), second)
    return even, odd


def send_rows_kernel(cols_ref, p_ref, before_ref, after_ref):
    rows = p_ref.shape[0] // 3
    width = p_ref.shape[1]
    half = width // 2
    mine = lax.axis_index("blk")
    place_row, _ = places(cols_ref, mine, rows)
    place = own_lanes(place_row, mine, rows)
    codes = [[], [], []]
    for first in (0, rows - RATIO):
        member = place - first
        good = (member >= 0) & (member < RATIO)
        none = jnp.full((8, 128), -1.0, F32)
        mem = jnp.where(good, member, none)
        nxt = jnp.where(good, member + RATIO, none)
        codes[0].append(three_wide((mem, nxt, none), rows))
        codes[1].append(three_wide((none, none, mem), rows))
        codes[2].append(three_wide((none, none, nxt), rows))
    picks = [jnp.concatenate([onehot(c[0:1, : 3 * rows], 8) for c in pair], axis=0) for pair in codes]
    left = dot(jnp.concatenate([picks[0], picks[1]], axis=0), p_ref[:, :half])
    right = dot(jnp.concatenate([picks[0], picks[2]], axis=0), p_ref[:, half:])
    for side, ref in ((0, before_ref), (1, after_ref)):
        at = 8 * side
        ref[:, :half] = left[at : at + 8].astype(BF16)
        ref[:, half:width] = right[at : at + 8].astype(BF16)
        ref[:, width:] = (left[16 + at : 24 + at] + right[16 + at : 24 + at]).astype(BF16)


def spread_rows(flat, work_ref, out_ref, row0, count, tile_count):
    per = count * 8
    highs = flat.shape[1] // 128
    for high in range(highs):
        work_ref[high * per : (high + 1) * per, :] = flat[:, high * 128 : (high + 1) * 128]
    for j in range(count):
        for tile in range(tile_count):
            first = work_ref[pl.ds(j * 8 + 2 * tile, highs, stride=per), :]
            second = work_ref[pl.ds(j * 8 + 2 * tile + 1, highs, stride=per), :]
            even, odd = swap_halves(first, second)
            out_ref[tile, pl.ds(row0 + j * 64, highs, stride=2), :] = even
            out_ref[tile, pl.ds(row0 + j * 64 + 1, highs, stride=2), :] = odd


def merge_kernel(smem_cols, cols_ref, acols_ref, p_ref, a_ref, lhs_ref, z_ref, pt_ref, halo_ref,
                 buf, place_smem, count_smem, sel, psel, work, zf, sems):
    rows, ka, width = a_ref.shape
    group = cols_ref.shape[1]
    coarse = rows // RATIO
    quads = rows // 8
    mine = lax.axis_index("blk")

    for c in range(coarse):
        count_smem[c] = 0

    def order(f, carry):
        agg = smem_cols[0, mine * rows + f] - mine * coarse
        at = count_smem[agg]
        count_smem[agg] = at + 1
        pltpu.make_async_copy(a_ref.at[f], buf.at[agg * RATIO + at, pl.ds(0, ka), :], sems.at[agg // 2]).start()
        return carry

    lax.fori_loop(0, rows, order, 0)
    buf[:, ka:, :] = jnp.zeros((rows, 32 - ka, width), BF16)

    place_row, place_col = places(cols_ref, mine, rows)
    col_rel = column_rel(cols_ref, mine, coarse)
    first = ((mine - 1) * rows).astype(F32)

    span = rows * 32
    rel = acols_ref[...].astype(F32) - first
    rel = jnp.where(rel < 0, rel + group, rel)
    rel = jnp.where(rel >= group, rel - group, rel)
    place_smem[...] = jnp.broadcast_to(place_col, (group, 128))
    own_col = place_smem[pl.ds(pl.multiple_of(mine * rows, 8), rows), :][:, 0:1]
    lane_row = iota((rows, span), 1) // 32
    to_lane = jnp.where(own_col == lane_row.astype(F32), 1.0, 0.0).astype(BF16)
    wide = dot(rel.astype(BF16), to_lane)
    k_lane = iota((ka, span), 1) % 32
    far = rows_sum(jnp.where(iota((ka, span), 0) == k_lane, wide, 0.0))
    rel_w = iota((group, 1), 0).astype(F32) - first
    rel_w = jnp.where(rel_w < 0, rel_w + group, rel_w)
    rel_w = jnp.where(rel_w >= group, rel_w - group, rel_w)
    far_place = rows_sum(jnp.where(rel_w == far, place_col, 0.0))
    lane = iota((1, span), 1)
    code = (far_place - (8 * (lane // 256) - RATIO).astype(F32)) * 8 + ((lane // 32) % 8).astype(F32)
    code = jnp.where(lane % 32 < ka, code, -1.0)
    for q in range(quads):
        sel[q] = onehot(code[:, q * 256 : (q + 1) * 256], 128)

    place = own_lanes(place_row, mine, rows).astype(jnp.int32)
    z_codes, t_codes = [], []
    for m in range(3):
        col = own_lanes(col_rel[m : m + 1], mine, rows).astype(jnp.int32)
        pair = (place + RATIO) // 8
        z_codes.append((pair * 64 + (place + RATIO) % 8 * 8 + col + 3 - 2 * pair).astype(F32))
        q = place // 8
        t_codes.append((q * 48 + (col + 2 - 2 * q) * 8 + place % 8).astype(F32))
    z_code = three_wide(z_codes, rows)[0:1, : 3 * rows]
    t_code = three_wide(t_codes, rows)[0:1, : 3 * rows]
    z_pick = onehot(z_code, (quads + 1) * 64)
    psel[...] = onehot(t_code, quads * 48)

    diag = iota((group, group), 0) == iota((group, group), 1)
    col_cols = [lanes_sum(jnp.where(diag, jnp.broadcast_to(col_rel[m : m + 1], (group, group)), 0.0)) for m in range(3)]
    r = iota((1, 16), 1)
    r_m = jnp.where(r < 8, r // RATIO, 2)
    r_i = r % RATIO
    for side, (start, shift) in enumerate(((-RATIO, 3), (rows, 3 - coarse))):
        hit = place_col == (r_i + start).astype(F32)
        slot = jnp.zeros((1, 16), F32)
        for m in range(3):
            slot = jnp.where(r_m == m, rows_sum(jnp.where(hit, col_cols[m], 0.0)), slot)
        row_code = (r_i * 8 + shift).astype(F32) + slot
        for part in range(2):
            keep = (r < 8) | (((r % 8) // RATIO) == part)
            halo_ref[side, part] = onehot(jnp.where(keep, row_code, -1.0), 32)

    for pair in range(quads + 1):
        flat = dot(z_pick[pair * 64 : (pair + 1) * 64], p_ref[...])
        spread_rows(flat, work, zf, 0, 8, 3)
        for tile in range(3):
            z_ref[pair, :, tile * 128 : (tile + 1) * 128] = zf[tile].astype(BF16)

    for q in range(quads):
        for _ in range(8):
            pltpu.make_async_copy(a_ref.at[0], buf.at[0, pl.ds(0, ka), :], sems.at[q]).wait()

        def chunk(step, carry):
            lanes = pl.ds(pl.multiple_of(step * 256, 256), 256)
            source = buf[q * 8 : (q + 1) * 8, :, lanes].reshape(256, 256)
            got = dot(sel[q], source)
            own = dot(psel[q * 48 : (q + 1) * 48, :], p_ref[:, lanes])
            at = pl.multiple_of(step * 16, 16)
            for values, ref, pairs in ((got, lhs_ref, 8), (own, pt_ref, 3)):
                for t in range(pairs):
                    a, b = (
                        jnp.concatenate([values[(2 * t + w) * 8 : (2 * t + w + 1) * 8, h * 128 : (h + 1) * 128]
                                         for h in range(2)], axis=0)
                        for w in range(2)
                    )
                    even, odd = swap_halves(a, b)
                    ref[q, pl.ds(at, 16), t * 128 : (t + 1) * 128] = even.astype(BF16)
                    ref[q, pl.ds(at + 256, 16), t * 128 : (t + 1) * 128] = odd.astype(BF16)
            return carry

        lax.fori_loop(0, width // 256, chunk, 0, unroll=2)


def second_product(pt, ap):
    return lax.dot_general(pt, ap, (((0,), (0,)), ((), ())), preferred_element_type=F32)


def blocks_of(acc_ref, row0, put):
    for tile in range(acc_ref.shape[0]):
        even = acc_ref[tile, pl.ds(row0, 32, stride=2), :]
        odd = acc_ref[tile, pl.ds(row0 + 1, 32, stride=2), :]
        first, second = swap_halves(even, odd)
        put(2 * tile, first)
        put(2 * tile + 1, second)


def edge_kernel(halo_ref, before_ref, after_ref, lhs_ref, z_ref, pt_ref, to_before, to_after, acc_ref,
                work, zf, zb, ap, part):
    quads = pt_ref.shape[0]
    width = before_ref.shape[1] // 3 * 2
    half = width // 2
    last = quads - 1
    band = to_before.shape[0] // 32
    for side, ref in ((0, before_ref), (1, after_ref)):
        pieces = []
        for h in range(2):
            pick = halo_ref[side, h]
            pieces.append(dot(pick[:, 0:8], ref[:, h * half : (h + 1) * half]) + dot(pick[:, 8:16], ref[:, width:]))
        flat = jnp.concatenate(pieces, axis=1)
        spread_rows(flat, work, zf, 0, 4, 3)
        for tile in range(3):
            zb[side, :, tile * 128 : (tile + 1) * 128] = zf[tile].astype(BF16)
    acc_ref[...] = jnp.zeros(acc_ref.shape, F32)
    for side, q in ((0, 0), (1, last)):
        lhs = lhs_ref.at[q]
        for at in range(0, 512, 128):
            rows = slice(at, at + 128)
            if side == 0:
                low = dot(lhs[rows, 0:256], zb[0]) + dot(lhs[rows, 256:512], z_ref[0, 256:512])
                high = dot(lhs[rows, 512:1024], z_ref[1])
            else:
                low = dot(lhs[rows, 0:512], z_ref[last])
                high = dot(lhs[rows, 512:768], z_ref[last + 1, 0:256]) + dot(lhs[rows, 768:1024], zb[1])
            ap[rows, 0:128] = low[:, 0:128].astype(BF16)
            ap[rows, 128:384] = (low[:, 128:] + high[:, :256]).astype(BF16)
            ap[rows, 384:512] = high[:, 256:].astype(BF16)
        product = second_product(pt_ref[q], ap[...])
        for tile in range(4):
            part[tile] = product[:, tile * 128 : (tile + 1) * 128]
        out_ref = (to_before, to_after)[side]
        for n, i in enumerate((0, 1) if side == 0 else (4, 5)):
            slots = range(4 - i, 11) if side == 0 else range(0, 12 - i)
            base = (0, 7)[n] if side == 0 else (0, 8)[n]

            def put(x, block):
                slot = x - i + 4
                if slot in slots:
                    at = (base + slot - slots[0]) * 32
                    out_ref[at : at + 32, :] = block.astype(BF16)

            blocks_of(part, i * 64, put)
        row0, acc0 = (128, 0) if side == 0 else (0, acc_ref.shape[1] - 256)
        acc_ref[q : q + 4, acc0 : acc0 + 256, :] = part[:, row0 : row0 + 256, :]


def inner_kernel(lhs_ref, z_ref, pt_ref, edge_ref, own_ref, acc, ap):
    quads = pt_ref.shape[0]
    coarse = own_ref.shape[0]
    band = own_ref.shape[1] // 32
    acc[...] = edge_ref[...]
    for q in range(1, quads - 1):
        lhs = lhs_ref.at[q]
        for at in range(0, 512, 128):
            rows = slice(at, at + 128)
            low = dot(lhs[rows, 0:512], z_ref[q])
            high = dot(lhs[rows, 512:1024], z_ref[q + 1])
            ap[rows, 0:128] = low[:, 0:128].astype(BF16)
            ap[rows, 128:384] = (low[:, 128:] + high[:, :256]).astype(BF16)
            ap[rows, 384:512] = high[:, 256:].astype(BF16)
        at = (2 * q - 2) * 64
        product = second_product(pt_ref[q], ap[...])
        for tile in range(4):
            acc[q + tile, at : at + 384, :] += product[:, tile * 128 : (tile + 1) * 128]
    for c in range(coarse):
        for slot in (s for s in range(band) if not 0 <= c + s - 2 < acc.shape[0] * 2):
            own_ref[c, slot * 32 : slot * 32 + 32, :] = jnp.zeros((32, 128), BF16)

        def put(x, block):
            slot = x - c + 2
            if 0 <= slot < band:
                own_ref[c, slot * 32 : slot * 32 + 32, :] = block.astype(BF16)

        blocks_of(acc, c * 64, put)


def reduce_kernel(owner_ref, own_ref, before_ref, after_ref, out_ref):
    coarse, rows, _ = own_ref.shape
    me = lax.axis_index("grp")
    count = out_ref.shape[0]
    if count > coarse:
        for h in range(count):
            out_ref[h] = jnp.zeros(out_ref.shape[1:], BF16)
    for c in range(coarse):
        target = owner_ref[0, me, c]
        if c < 2:
            at, size, base = 0, (8 - c) * 32, 8 * 32 * c
            extra = before_ref[base : base + size, :]
        elif c >= coarse - 2:
            n = c - (coarse - 2)
            size, base = (7 + n) * 32, 7 * 32 * n
            at = rows - size
            extra = after_ref[base : base + size, :]
        else:
            size = 0
        if size == 0:
            out_ref[target] = own_ref[c]
            continue
        if at > 0:
            out_ref[target, 0:at, :] = own_ref[c, 0:at, :]
        if at + size < rows:
            out_ref[target, at + size :, :] = own_ref[c, at + size :, :]
        total = own_ref[c, at : at + size, :].astype(F32) + extra.astype(F32)
        out_ref[target, at : at + size, :] = total.astype(BF16)


def place_kernel(in_ref, out_ref, work):
    count, rows, _ = in_ref.shape
    band = rows // 32
    for q in range(count):
        work[q * rows : (q + 1) * rows, :] = in_ref[q].astype(F32)

    def one(s, carry):
        for h in range(32):
            tile = work[pl.ds(s * 32 + h, count, stride=rows), :]
            out_ref[s, :, h * 128 : (h + 1) * 128] = tile.astype(BF16)
        return carry

    lax.fori_loop(0, band, one, 0)


VM = pl.BlockSpec(memory_space=pltpu.VMEM)
SM = pl.BlockSpec(memory_space=pltpu.SMEM)
ANY = pl.BlockSpec(memory_space=pl.ANY)


def call(kernel, outs, ins, scratch=(), flops=0, size=0):
    return pl.pallas_call(
        kernel,
        out_shape=[jax.ShapeDtypeStruct(s, d) for s, d in outs],
        in_specs=ins,
        out_specs=[VM] * len(outs),
        scratch_shapes=list(scratch),
        compiler_params=pltpu.CompilerParams(vmem_limit_bytes=LIMIT),
        cost_estimate=pl.CostEstimate(flops=flops, bytes_accessed=size, transcendentals=0),
    )


def body(a_blocks, a_cols, p_blocks, p_cols, owner):
    rows, ka, width = a_blocks.shape
    group = p_cols.shape[0]
    coarse = rows // RATIO
    quads = rows // 8
    band = 11
    blks, grps = lax.axis_size("blk"), lax.axis_size("grp")
    cols_t = p_cols.T
    acols_t = a_cols.T
    p_flat = jnp.transpose(p_blocks, (1, 0, 2)).reshape(3 * rows, width)
    tail = width // 2 * 3
    to_before, to_after = call(send_rows_kernel, [((8, tail), BF16)] * 2, [VM, VM], size=1 << 20)(cols_t, p_flat)
    up = [(i, (i + 1) % blks) for i in range(blks)]
    down = [((i + 1) % blks, i) for i in range(blks)]
    p_before = lax.ppermute(to_after, "blk", up)
    p_after = lax.ppermute(to_before, "blk", down)
    lhs, z, pt, halo = call(
        merge_kernel,
        [((quads, 512, 1024), BF16), ((quads + 1, 512, 384), BF16), ((quads, 512, 384), BF16), ((2, 2, 32, 16), BF16)],
        [SM, VM, VM, VM, ANY],
        [
            pltpu.VMEM((rows, 32, width), BF16),
            pltpu.VMEM((group, 128), F32),
            pltpu.SMEM((coarse,), jnp.int32),
            pltpu.VMEM((quads, 128, 256), BF16),
            pltpu.VMEM((quads * 48, 3 * rows), BF16),
            pltpu.VMEM((32 * 64, 128), F32),
            pltpu.VMEM((3, 512, 128), F32),
            pltpu.SemaphoreType.DMA((quads,)),
        ],
        flops=4 << 30, size=16 << 20,
    )(cols_t, cols_t, acols_t, p_flat, a_blocks)
    send_before, send_after, edge = call(
        edge_kernel,
        [((15 * 32, 128), BF16)] * 2 + [((quads + 3, coarse * 64, 128), F32)],
        [VM] * 6,
        [
            pltpu.VMEM((32 * 32, 128), F32),
            pltpu.VMEM((3, 256, 128), F32),
            pltpu.VMEM((2, 256, 384), BF16),
            pltpu.VMEM((512, 512), BF16),
            pltpu.VMEM((4, 384, 128), F32),
        ],
        flops=1 << 30, size=4 << 20,
    )(halo, p_before, p_after, lhs, z, pt)
    from_before = lax.ppermute(send_after, "blk", up)
    from_after = lax.ppermute(send_before, "blk", down)
    (own,) = call(
        inner_kernel,
        [((coarse, band * 32, 128), BF16)],
        [VM] * 4,
        [pltpu.VMEM((quads + 3, coarse * 64, 128), F32), pltpu.VMEM((512, 512), BF16)],
        flops=2 << 30, size=8 << 20,
    )(lhs, z, pt, edge)
    (outgoing,) = call(
        reduce_kernel, [((grps, band * 32, 128), BF16)], [SM, VM, VM, VM], size=2 << 20
    )(owner, own, from_before, from_after)
    arrived = lax.all_to_all(outgoing, "grp", split_axis=0, concat_axis=0, tiled=True)
    (placed,) = call(
        place_kernel, [((band, grps, width), BF16)], [VM], [pltpu.VMEM((grps * band * 32, 128), F32)], size=2 << 20
    )(arrived)
    return jnp.transpose(placed, (1, 0, 2))


def solution(mesh):
    return jax.shard_map(
        body,
        mesh=mesh,
        in_specs=(
            P(("grp", "blk"), None, None),
            P(("grp", "blk"), None),
            P(("grp", "blk"), None, None),
            P("grp", None),
            P("blk", None, None),
        ),
        out_specs=P(("grp", "blk"), None, None),
        check_vma=False,
    )
```

time: 207 us -> 52.5 us (0.25)
  local copies, waits for them, and re-layouts: 88.2 us -> 3.66 us
  matrix products: 53 us -> 0 us
  waiting for transfers between devices: 29.5 us -> 2.18 us
  Pallas kernels: 0 us -> 21.9 us
  other arithmetic: 7.52 us -> 0 us
  blocking collectives: 18.8 us -> 15.3 us
    dot_general x6 -> x0, matrix products: 53 us -> none  [the longest x1 18.5 us: body(): jnp.einsum('cidtab,cdtsbx->cidsax', a_ordered, p_window.astype(jnp.float3...]
    ppermute x4, waiting for transfers between devices: 29.5 us -> 2.18 us  [the longest x1 2.18 us: body(): from_before = lax.ppermute(send_after, 'blk', up)]
    another operation x6 -> x0, local copies, waits for them, and re-layouts: 22.3 us -> none  [body(): jnp.stack([ordered[coarse_dev - 1 + near:2 * coarse_dev - 1 + near] for n...]
    pallas_call x0 -> x6, Pallas kernels: none -> 21.9 us  [the longest x1 14.4 us: body(): call(merge_kernel, [((quads, 512, 1024), BF16), ((quads + 1, 512, 384), B...]
    reshape x2 -> x0, local copies, waits for them, and re-layouts: 19.1 us -> none  [the longest x1 10.9 us: body(): a_ordered = a_ordered.reshape(coarse_dev, RATIO, 3, RATIO, B, B)]
    squeeze x2 -> x0, local copies, waits for them, and re-layouts: 15.1 us -> none  [the longest x1 12.5 us: body(): products[:, :, 0]]
    transpose x1 -> x0, local copies, waits for them, and re-layouts: 10.9 us -> none  [body(): jnp.einsum('cisbu,ciebv->cseuv', own_p, ap_rows, preferred_element_type=j...]
    gather x4 -> x0, local copies, waits for them, and re-layouts: 9.73 us -> none  [the longest x2 4.87 us: body(): far_member = member[far_rows]]
  transfers between devices with their start and end apart: 4 -> 4, of which waited for: 2 -> 1; matrix products, arithmetic and copies ran while one was open for 18% -> 0% of each run, Pallas kernels for 0% -> 31%
where the time goes in v1:
time: 52.5 us; the launch traced here: 52.2 us
  Pallas kernels  21.9 us (42%)
  blocking collectives  15.3 us (29%)
  starting transfers between devices  9.07 us (17%)
  local copies, waits for them, and re-layouts  3.66 us (7%)
  waiting for transfers between devices  2.18 us (4%)
    all_to_all x1, blocking collectives, body(): lax.all_to_all(outgoing, 'grp', split_axis=0, concat_axis=0, tiled=True)  15.3 us
    pallas_call x1, Pallas kernels, body(): call(merge_kernel, [((quads, 512, 1024), BF16), ((quads + 1, 512, 384), B...  14.4 us
    ppermute x1, starting transfers between devices, body(): from_after = lax.ppermute(send_before, 'blk', down)  3.81 us
    unnamed x10, local copies, waits for them, and re-layouts  3.66 us
    ppermute x1, starting transfers between devices, body(): p_before = lax.ppermute(to_after, 'blk', up)  3.1 us
    pallas_call x1, Pallas kernels, body(): call(edge_kernel, [((15 * 32, 128), BF16)] * 2 + [((quads + 3, coarse * 6...  2.58 us
    ppermute x1, waiting for transfers between devices, body(): from_before = lax.ppermute(send_after, 'blk', up)  2.18 us
    ppermute x1, starting transfers between devices, body(): p_after = lax.ppermute(to_before, 'blk', down)  2.09 us
  transfers between devices with their start and end apart: 4, of which 1 were waited for; matrix products, arithmetic and copies ran while one was open for 0% of the time, Pallas kernels for 31%

profile of v1, /device:TPU:0, one launch (start us, length us, event | category | flops | bytes accessed | tf_op | source)
XLA Modules:
  0.0 52.2 jit_solution(13335880497139050578)
XLA Ops:
  0.0 0.0 copy-start
  0.0 1.1 %copy-done = bf16[32,3,4096]{2,0,1:T(8,128)(2,1)S(1)} copy-done((bf16[32,3,4096]{2,0,1:T(8,128)(2,1)S(1)}, bf16[32,3,4096]{2,0,1:T(8,128)(2,1)}, u32[]{:S(2)}) %copy-start) | copy-done | bytes 786456
  1.1 0.0 copy-start.3
  1.1 0.7 %copy-done.3 = s32[128,3]{0,1:T(4,128)S(1)} copy-done((s32[128,3]{0,1:T(4,128)S(1)}, s32[128,3]{0,1:T(4,128)}, u32[]{:S(2)}) %copy-start.3) | copy-done | bytes 1560
  1.8 0.5 shard_map.56
  2.3 3.1 %collective-permute-start = (bf16[8,6144]{1,0:T(8,128)(2,1)S(1)}, bf16[8,6144]{1,0:T(8,128)(2,1)S(1)}, u32[]{:S(2)}, u32[]{:S(2)}) collective-permute-start(bf16[8,6144]{1,0:T(8,128)(2,1)S(1)} %get-tuple-element.18), channel_id=1, source_target_pairs={{0,1},{1,2},{2,3},{3,0},{4,5},{5,6},{6,7},{7,4},{8,9},{9,10},{10,1... | collective-permute-start | bytes 294920 | tf_op jit(solution)/shard_map/ppermute | solution.py:403
  5.4 2.1 %collective-permute-start.1 = (bf16[8,6144]{1,0:T(8,128)(2,1)S(1)}, bf16[8,6144]{1,0:T(8,128)(2,1)S(1)}, u32[]{:S(2)}, u32[]{:S(2)}) collective-permute-start(bf16[8,6144]{1,0:T(8,128)(2,1)S(1)} %get-tuple-element.19), channel_id=1, source_target_pairs={{1,0},{2,1},{3,2},{0,3},{5,4},{6,5},{7,6},{4,7},{9,8},{10,9},{11,1... | collective-permute-start | bytes 294920 | tf_op jit(solution)/shard_map/ppermute | solution.py:404
  7.5 0.0 copy-start.1
  7.5 1.1 %copy-done.1 = bf16[32,3,4096]{2,0,1:T(8,128)(2,1)S(1)} copy-done((bf16[32,3,4096]{2,0,1:T(8,128)(2,1)S(1)}, bf16[32,3,4096]{2,0,1:T(8,128)(2,1)}, u32[]{:S(2)}) %copy-start.1) | copy-done | bytes 786456
  8.6 0.0 copy-start.4
  8.6 0.7 %copy-done.4 = s32[32,24]{0,1:T(8,128)S(1)} copy-done((s32[32,24]{0,1:T(8,128)S(1)}, s32[32,24]{0,1:T(8,128)}, u32[]{:S(2)}) %copy-start.4) | copy-done | bytes 3096
  9.3 14.4 %shard_map.55 = (bf16[4,512,1024]{2,1,0:T(8,128)(2,1)S(1)}, bf16[5,512,384]{2,1,0:T(8,128)(2,1)S(1)}, bf16[4,512,384]{2,1,0:T(8,128)(2,1)S(1)}, bf16[2,2,32,16]{3,2,1,0:T(8,128)(2,1)S(1)}) custom-call(s32[3,128]{1,0:T(4,128)S(1)} %bitcast.9, s32[3,128]{1,0:T(4,128)S(1)} %bitcast.10, s32[24,32]{1,0:T(8,128)S(1)} %bitcast.11, bf16[96,4096]{1,0:T(8,128)(2,1)S(1)} %bitcast.7, ...), custom_call_target="tpu_custom_call" | custom-call | flops 4294967296 | bytes 16777216 | tf_op jit(solution)/shard_map/pallas_call | solution.py:405
  23.7 0.0 collective-permute-done.before_ref
  23.7 0.0 collective-permute-done.1.after_ref
  23.7 2.6 %shard_map.57 = (bf16[480,128]{1,0:T(8,128)(2,1)S(1)}, bf16[480,128]{1,0:T(8,128)(2,1)S(1)}, f32[7,512,128]{2,1,0:T(8,128)S(1)}) custom-call(bf16[2,2,32,16]{3,2,1,0:T(8,128)(2,1)S(1)} %get-tuple-element.17.halo_ref, bf16[8,6144]{1,0:T(8,128)(2,1)S(1)} %collective-permute-done.before_ref, bf16[8,6144]{1,0:T(8,128)(2,1)S(1)} %collective-permute-done.1.after_ref, ...), custom_call_target="tpu_custom_call" | custom-call | flops 1073741824 | bytes 4194304 | tf_op jit(solution)/shard_map/pallas_call | solution.py:421
  26.3 0.1 collective-permute-start.2
  26.4 3.8 %collective-permute-start.3 = (bf16[480,128]{1,0:T(8,128)(2,1)S(1)}, bf16[480,128]{1,0:T(8,128)(2,1)S(1)}, u32[]{:S(2)}, u32[]{:S(2)}) collective-permute-start(bf16[480,128]{1,0:T(8,128)(2,1)S(1)} %get-tuple-element.22), channel_id=1, source_target_pairs={{1,0},{2,1},{3,2},{0,3},{5,4},{6,5},{7,6},{4,7},{9,8},{10,9},{11,1... | collective-permute-start | bytes 368648 | tf_op jit(solution)/shard_map/ppermute | solution.py:435
  30.2 1.9 %shard_map.58.own_ref = bf16[8,352,128]{2,1,0:T(8,128)(2,1)S(1)} custom-call(bf16[4,512,1024]{2,1,0:T(8,128)(2,1)S(1)} %get-tuple-element.14.lhs_ref, bf16[5,512,384]{2,1,0:T(8,128)(2,1)S(1)} %get-tuple-element.15.z_ref, bf16[4,512,384]{2,1,0:T(8,128)(2,1)S(1)} %get-tuple-element.16.pt_ref, f32[7,512,128]{2,1,0:T(8,128)S(1)} %get-tuple-element.20.edge_ref), custom_call_target="tpu_custom_call" | custom-call | flops 2147483648 | bytes 8388608 | tf_op jit(solution)/shard_map/pallas_call | solution.py:436
  32.1 2.2 %collective-permute-done.2.before_ref = bf16[480,128]{1,0:T(8,128)(2,1)S(1)} collective-permute-done((bf16[480,128]{1,0:T(8,128)(2,1)S(1)}, bf16[480,128]{1,0:T(8,128)(2,1)S(1)}, u32[]{:S(2)}, u32[]{:S(2)}) %collective-permute-start.2) | collective-permute-done | bytes 122912 | tf_op jit(solution)/shard_map/ppermute | solution.py:434
  34.3 0.0 collective-permute-done.3.after_ref
  34.3 0.0 copy-done.2
  34.3 0.7 %shard_map.59 = bf16[8,352,128]{2,1,0:T(8,128)(2,1)S(1)} custom-call(s32[1,8,8]{2,1,0:T(8,128)S(1)} %copy-done.2, bf16[8,352,128]{2,1,0:T(8,128)(2,1)S(1)} %shard_map.58.own_ref, bf16[480,128]{1,0:T(8,128)(2,1)S(1)} %collective-permute-done.2.before_ref, bf16[480,128]{1,0:T(8,128)(2,1)S(1)} %collective-permute-done.3.after_ref), custom_call_target="tpu_custom_call" | custom-call | bytes 2097152 | tf_op jit(solution)/shard_map/pallas_call | solution.py:443
  35.0 15.3 %all_to_all.5.in_ref = bf16[8,352,128]{2,1,0:T(8,128)(2,1)S(1)} all-to-all(bf16[8,352,128]{2,1,0:T(8,128)(2,1)S(1)} %shard_map.59), channel_id=1, replica_groups=mesh['grp'=8,'blk'=4] {'grp'}, dimensions={0} | all-to-all | bytes 1441792 | tf_op jit(solution)/shard_map/all_to_all | solution.py:446
  50.3 1.9 %shard_map.60 = bf16[11,8,4096]{2,1,0:T(8,128)(2,1)} custom-call(bf16[8,352,128]{2,1,0:T(8,128)(2,1)S(1)} %all_to_all.5.in_ref), custom_call_target="tpu_custom_call" | custom-call | bytes 2097152 | tf_op jit(solution)/shard_map/pallas_call | solution.py:447
  (1 shorter events, 0.0 us)
Async XLA Ops:
  0.0 1.1 %copy-start = (bf16[32,3,4096]{2,0,1:T(8,128)(2,1)S(1)}, bf16[32,3,4096]{2,0,1:T(8,128)(2,1)}, u32[]{:S(2)}) copy-start(bf16[32,3,4096]{2,0,1:T(8,128)(2,1)} %param.7) | copy-start | bytes 2359300
  1.1 0.7 %copy-start.3 = (s32[128,3]{0,1:T(4,128)S(1)}, s32[128,3]{0,1:T(4,128)}, u32[]{:S(2)}) copy-start(s32[128,3]{0,1:T(4,128)} %param.8) | copy-start | bytes 4612
  2.3 21.4 %collective-permute-start = (bf16[8,6144]{1,0:T(8,128)(2,1)S(1)}, bf16[8,6144]{1,0:T(8,128)(2,1)S(1)}, u32[]{:S(2)}, u32[]{:S(2)}) collective-permute-start(bf16[8,6144]{1,0:T(8,128)(2,1)S(1)} %get-tuple-element.18), channel_id=1, source_target_pairs={{0,1},{1,2},{2,3},{3,0},{4,5},{5,6},{6,7},{7,4},{8,9},{9,10},{10,1... | collective-permute-start | bytes 294920 | tf_op jit(solution)/shard_map/ppermute | solution.py:403
  5.4 18.3 %collective-permute-start.1 = (bf16[8,6144]{1,0:T(8,128)(2,1)S(1)}, bf16[8,6144]{1,0:T(8,128)(2,1)S(1)}, u32[]{:S(2)}, u32[]{:S(2)}) collective-permute-start(bf16[8,6144]{1,0:T(8,128)(2,1)S(1)} %get-tuple-element.19), channel_id=1, source_target_pairs={{1,0},{2,1},{3,2},{0,3},{5,4},{6,5},{7,6},{4,7},{9,8},{10,9},{11,1... | collective-permute-start | bytes 294920 | tf_op jit(solution)/shard_map/ppermute | solution.py:404
  7.5 1.1 %copy-start.1 = (bf16[32,3,4096]{2,0,1:T(8,128)(2,1)S(1)}, bf16[32,3,4096]{2,0,1:T(8,128)(2,1)}, u32[]{:S(2)}) copy-start(bf16[32,3,4096]{2,0,1:T(8,128)(2,1)} %param.7) | copy-start | bytes 2359300
  8.6 0.7 %copy-start.4 = (s32[32,24]{0,1:T(8,128)S(1)}, s32[32,24]{0,1:T(8,128)}, u32[]{:S(2)}) copy-start(s32[32,24]{0,1:T(8,128)} %param.6) | copy-start | bytes 9220
  26.3 8.0 %collective-permute-start.2 = (bf16[480,128]{1,0:T(8,128)(2,1)S(1)}, bf16[480,128]{1,0:T(8,128)(2,1)S(1)}, u32[]{:S(2)}, u32[]{:S(2)}) collective-permute-start(bf16[480,128]{1,0:T(8,128)(2,1)S(1)} %get-tuple-element.21), channel_id=1, source_target_pairs={{0,1},{1,2},{2,3},{3,0},{4,5},{5,6},{6,7},{7,4},{8,9},{9,10},{10,1... | collective-permute-start | bytes 368648 | tf_op jit(solution)/shard_map/ppermute | solution.py:434
  26.4 7.9 %collective-permute-start.3 = (bf16[480,128]{1,0:T(8,128)(2,1)S(1)}, bf16[480,128]{1,0:T(8,128)(2,1)S(1)}, u32[]{:S(2)}, u32[]{:S(2)}) collective-permute-start(bf16[480,128]{1,0:T(8,128)(2,1)S(1)} %get-tuple-element.22), channel_id=1, source_target_pairs={{1,0},{2,1},{3,2},{0,3},{5,4},{6,5},{7,6},{4,7},{9,8},{10,9},{11,1... | collective-permute-start | bytes 368648 | tf_op jit(solution)/shard_map/ppermute | solution.py:435
  30.2 4.1 %copy-start.2 = (s32[1,8,8]{2,1,0:T(8,128)S(1)}, s32[1,8,8]{2,1,0:T(8,128)}, u32[]{:S(2)}) copy-start(s32[1,8,8]{2,1,0:T(8,128)} %owner_ref.1) | copy-start | bytes 772
